TPU v7x, 512 devices: a whole 4x8x8 slice. The times are simulated.
512 devices in a mesh: pb: 32 (over z, x), ka: 16 (over y, core).
Axes of the slice: x: 4, y: 8, z: 8, core: 2. Of those that a mesh axis runs over, the one named last changes fastest.
Arguments:
- features: bfloat16 [65536, 1024], P(('pb', 'ka')), may hold values from -8.5 to 8.5
- order: int32 [65536], P(('pb', 'ka')), may hold values from 0 to 127, as said below
- neighbours: int32 [512, 24], P('pb'), may hold values from 0 to 511, as said below
- counts: int32 [512], P('pb'), may hold values from 1 to 24, as said below
- qkv_weight: bfloat16 [1024, 1536], P(('pb', 'ka')), may hold values from -0.25 to 0.25
- out_weight: bfloat16 [512, 1024], P(None, ('pb', 'ka')), may hold values from -1 to 1
Outputs:
- mixed: bfloat16 [65536, 1024], P(('pb', 'ka'))
Inputs may be any that keep to these rules, and one draw needn't show every extreme that they name: `order`: each aligned group of 128 entries is a permutation of 0 to 127. `neighbours`: entry 0 of the list of block a is a itself; the first counts[a] entries are distinct and lie in a's slab of 16 blocks or in the slabs just before and after it, cyclically; slots from counts[a] on hold some block id and are not part of the list. `counts`: some block's list fills all 24 slots.
All inputs are finite; a program needn't handle non-finite values.
Results may differ from a plain program's by a relative error of at most 0.012.
The roundings to bfloat16 on the way count: a program that leaves them out, or rounds other values in their place, can miss the bound.
Values may be sent and summed in bfloat16 or wider, within the bound.
No kernel may reach another device: no remote copies, remote signals or barrier semaphores. Data moves between devices by JAX's collectives and lax.ppermute only.
A program may use at most 64 MiB of HBM per device.

v0:
```python
import jax
import jax.numpy as jnp
from jax import lax
from jax.sharding import PartitionSpec as P

HD = 64
BLK = 128


def padded(array, sides, width):
    for axis, dim in sides:
        size, length = (lax.axis_size(axis), array.shape[dim])
        up = [(i, (i + 1) % size) for i in range(size)]
        down = [(j, i) for i, j in up]
        last = lax.slice_in_dim(array, length - width, length, axis=dim)
        leading = lax.slice_in_dim(array, 0, width, axis=dim)
        before = lax.ppermute(last, axis, up)
        after = lax.ppermute(leading, axis, down)
        array = jnp.concatenate([before, array, after], axis=dim)
    return array


def attend_rows(query_rows, allow_rows, near_keys, near_values, score_scale):
    row_total = query_rows.shape[0]
    head_count = query_rows.shape[1]
    attn_width = head_count * query_rows.shape[2]
    tile_rows = 512
    tile_count = row_total // tile_rows

    def attend(tile_args):
        query_tile, allow_tile = tile_args
        allowed = jnp.repeat(allow_tile, BLK, axis=1)
        scores = (
            jnp.einsum("qhd,khd->hqk", query_tile, near_keys, preferred_element_type=jnp.float32)
            * score_scale
        )
        row_max = jnp.max(jnp.where(allowed[None], scores, -1e30), axis=-1)
        row_shift = row_max.astype(jnp.bfloat16)
        soft_weights = jnp.where(
            allowed[None], jnp.exp(scores - row_shift.astype(jnp.float32)[..., None]), 0.0
        )
        group_total = jnp.sum(soft_weights, axis=-1).T
        numerator = jnp.einsum(
            "hqk,khd->qhd",
            soft_weights.astype(jnp.bfloat16),
            near_values,
            preferred_element_type=jnp.float32,
        )
        positive = group_total > 0
        partial_value = jnp.where(
            positive[..., None], numerator / jnp.where(positive, group_total, 1.0)[..., None], 0.0
        )
        return (
            partial_value.astype(jnp.bfloat16).reshape(tile_rows, attn_width),
            row_shift.T,
            group_total.astype(jnp.bfloat16),
        )

    tiled = lax.map(
        attend,
        (
            query_rows.reshape(tile_count, tile_rows, head_count, query_rows.shape[2]),
            allow_rows.reshape(tile_count, tile_rows, -1),
        ),
    )
    return (
        tiled[0].reshape(row_total, attn_width),
        tiled[1].reshape(row_total, head_count),
        tiled[2].reshape(row_total, head_count),
    )


def body(features, order, neighbours, counts, qkv_weight, out_weight):
    dev_rows = features.shape[0]
    sorted_rows = jnp.take(features, order, axis=0)
    attn_width = qkv_weight.shape[1] // 3
    head_count = attn_width // HD
    score_scale = HD ** (-0.5)
    projected = jnp.dot(
        sorted_rows,
        lax.all_gather(qkv_weight, ("pb", "ka"), axis=0, tiled=True),
        preferred_element_type=jnp.float32,
    )
    own_queries = projected[:, :attn_width].astype(jnp.bfloat16)
    keys_values = projected[:, attn_width:].astype(jnp.bfloat16)
    near = padded(keys_values, (("pb", 0),), dev_rows)
    slab_index = lax.axis_index("pb")
    group_index = lax.axis_index("ka")
    slab_count = lax.axis_size("pb")
    group_count = lax.axis_size("ka")
    dev_blocks = dev_rows // BLK
    slab_of = (slab_index + jnp.arange(3) - 1) % slab_count
    listed_slot = jnp.arange(neighbours.shape[1])[None, :] < counts[:, None]
    slab_queries = lax.all_gather(own_queries, "ka", axis=0, tiled=True)
    near_keys = near[:, :attn_width].reshape(3 * dev_rows, head_count, HD)
    near_values = near[:, attn_width:].reshape(3 * dev_rows, head_count, HD)
    block_ids = (
        (slab_of[:, None] * group_count + group_index) * dev_blocks
        + jnp.arange(dev_blocks)[None, :]
    ).reshape(-1)
    member = jnp.any(
        (neighbours[:, :, None] == block_ids[None, None, :]) & listed_slot[:, :, None], axis=1
    )
    row_member = jnp.repeat(member, BLK, axis=0)
    partial_value, row_shift, group_total = attend_rows(
        slab_queries.reshape(-1, head_count, HD), row_member, near_keys, near_values, score_scale
    )
    received = (
        lax.all_to_all(partial_value[None], "ka", split_axis=1, concat_axis=0, tiled=True),
        lax.all_to_all(row_shift[None], "ka", split_axis=1, concat_axis=0, tiled=True),
        lax.all_to_all(group_total[None], "ka", split_axis=1, concat_axis=0, tiled=True),
    )
    group_out = received[0].reshape(group_count, dev_rows, head_count, HD).astype(jnp.float32)
    group_max = received[1].astype(jnp.float32)
    total_rounded = received[2].astype(jnp.float32)
    top_shift = jnp.max(group_max, axis=0, keepdims=True)
    weight_g = total_rounded * jnp.exp(group_max - top_shift)
    combined = (
        jnp.sum(weight_g[..., None] * group_out, axis=0) / jnp.sum(weight_g, axis=0)[..., None]
    )
    attended = combined.reshape(dev_rows, attn_width).astype(jnp.bfloat16)
    mixed = jnp.dot(
        attended,
        lax.all_gather(out_weight, ("pb", "ka"), axis=1, tiled=True),
        preferred_element_type=jnp.float32,
    )
    return mixed.astype(jnp.bfloat16)


def solution(mesh):
    return jax.shard_map(
        body,
        mesh=mesh,
        in_specs=(
            P(("pb", "ka"), None),
            P(("pb", "ka")),
            P("pb", None),
            P("pb"),
            P(("pb", "ka"), None),
            P(None, ("pb", "ka")),
        ),
        out_specs=P(("pb", "ka"), None),
        check_vma=False,
    )
```

profile of v0, /device:TPU:1, one launch (start us, length us, event | category | flops | bytes accessed | tf_op | source)
XLA Modules:
  0.0 470.9 jit_solution(14192227212871008691)
XLA Ops:
  6.5 0.7 all-gather.8.cloned.1.call-update
  7.3 0.7 compare_select_fusion
  8.0 1.6 gather_fusion
  9.5 0.7 compare_and_fusion
  10.2 124.0 %all-gather.8.cloned.1.call-done = bf16[512,2,1536]{2,1,0:T(2,128)(2,1)} async-done(((bf16[1,2,1536]{2,1,0:T(2,128)(2,1)}), bf16[512,2,1536]{2,1,0:T(2,128)(2,1)}) %all-gather.8.cloned.1.call-update) | async-done | bytes 3145744 | tf_op jit(solution)/shard_map/all_gather | solution.py:81
  134.2 6.3 %reshape.136 = bf16[1024,1536]{1,0:T(8,128)(2,1)S(1)} reshape(bf16[512,2,1536]{2,1,0:T(2,128)(2,1)} %all-gather.8.cloned.1.call-done) | data formatting | bytes 6291456
  140.6 1.6 convolution_convert_fusion
  142.2 0.7 copy-done.2
  142.9 0.7 slice.20
  143.6 1.0 slice.21
  144.6 3.1 collective-permute-start
  147.6 5.7 %collective-permute-start.1 = (bf16[128,1024]{1,0:T(8,128)(2,1)S(1)}, bf16[128,1024]{1,0:T(8,128)(2,1)S(1)}, u32[]{:S(2)}, u32[]{:S(2)}) collective-permute-start(bf16[128,1024]{1,0:T(8,128)(2,1)S(1)} %slice.21), channel_id=1, source_target_pairs={{16,0},{32,16},{48,32},{64,48},{80,64},{96,80},{112,96},{128,112},... | collective-permute-start | bytes 786440 | tf_op jit(solution)/shard_map/ppermute | solution.py:18
  153.5 0.2 and_reduce_fusion
  153.8 3.6 collective-permute-done
  157.4 0.9 collective-permute-done.1
  158.8 22.9 %all-gather.6.cloned.1.call-done = bf16[2048,512]{1,0:T(8,128)(2,1)} async-done(((bf16[128,512]{1,0:T(8,128)(2,1)}), bf16[2048,512]{1,0:T(8,128)(2,1)}) %all-gather.6.cloned.1.call-update) | async-done | bytes 2097168 | tf_op jit(solution)/shard_map/all_gather | solution.py:94
  181.7 6.2 %reshape.139 = bf16[4,512,8,64]{3,2,1,0:T(8,128)(2,1)} reshape(bf16[2048,512]{1,0:T(8,128)(2,1)} %all-gather.6.cloned.1.call-done) | data formatting | bytes 4194304 | tf_op jit(solution)/shard_map/reshape;reshape | solution.py:62
  187.9 5.5 %copy.79 = bf16[4,512,8,64]{1,3,2,0:T(8,128)(2,1)} copy(bf16[4,512,8,64]{3,2,1,0:T(8,128)(2,1)} %reshape.139) | data formatting | bytes 4194304 | tf_op jit(solution)/shard_map/while | solution.py:59
  193.3 24.9 %while.14 = (s32[]{:T(128)}, bf16[4,512,512]{2,1,0:T(8,128)(2,1)}, bf16[4,512,8]{1,2,0:T(8,128)(2,1)S(1)}, bf16[4,512,8]{1,2,0:T(8,128)(2,1)S(1)}, pred[4,512,3]...) while((s32[]{:T(128)}, bf16[4,512,512]{2,1,0:T(8,128)(2,1)}, ...), condition=%wide.region_4.5_spmd, body=%wide.region_1.4_spmd.sunk | while | flops 420753408 | bytes 23795300 | solution.py:59
  193.4 2.2 select_reduce_fusion.2
  195.6 1.3 fusion.40
  197.0 1.5 select_convert_fusion.2
  198.5 0.2 copy.99
  198.7 0.8 constant_dynamic-update-slice_fusion.2
  199.6 2.2 select_reduce_fusion.2
  201.8 1.3 fusion.40
  203.2 1.5 select_convert_fusion.2
  204.7 0.2 copy.99
  204.9 0.9 constant_dynamic-update-slice_fusion.2
  205.8 2.2 select_reduce_fusion.2
  208.0 1.3 fusion.40
  209.4 1.5 select_convert_fusion.2
  211.1 0.8 constant_dynamic-update-slice_fusion.2
  212.0 2.2 select_reduce_fusion.2
  214.2 1.3 fusion.40
  215.6 1.5 select_convert_fusion.2
  217.3 0.9 constant_dynamic-update-slice_fusion.2
  218.2 0.7 copy.82
  218.9 0.5 broadcast.127
  219.4 12.2 %reduce.6 = bf16[2048,8]{1,0:T(8,128)(2,1)} reduce(bf16[2048,1,8]{2,1,0:T(2,128)(2,1)S(1)} %bitcast.101, bf16[]{:T(256)} %broadcast.127), dimensions={1}, to_apply=%bitcast.57.reduce_sub_computation | reduce | bytes 65538
  231.7 2.2 reshape.144
  233.8 4.9 %all-to-all-start.1 = ((bf16[16,2,512]{2,1,0:T(2,128)(2,1)}), bf16[16,2,512]{2,1,0:T(2,128)(2,1)S(1)}, u32[]{:S(2)}, u32[]{:S(2)}) async-start(bf16[16,2,512]{2,1,0:T(2,128)(2,1)} %reshape.144), calls=%async_computation.1 | async-start | bytes 65536 | tf_op jit(solution)/shard_map/all_to_all | solution.py:110
  238.7 0.7 copy.80
  239.5 12.2 %reduce.7 = bf16[2048,8]{1,0:T(8,128)(2,1)} reduce(bf16[2048,1,8]{2,1,0:T(2,128)(2,1)S(1)} %bitcast.102, bf16[]{:T(256)} %broadcast.127), dimensions={1}, to_apply=%bitcast.55.reduce_sub_computation | reduce | bytes 65538
  251.7 2.2 reshape.142
  253.9 7.2 %all-to-all-start = ((bf16[16,2,512]{2,1,0:T(2,128)(2,1)}), bf16[16,2,512]{2,1,0:T(2,128)(2,1)S(1)}, u32[]{:S(2)}, u32[]{:S(2)}) async-start(bf16[16,2,512]{2,1,0:T(2,128)(2,1)} %reshape.142), calls=%async_computation | async-start | bytes 65536 | tf_op jit(solution)/shard_map/all_to_all | solution.py:111
  261.1 18.5 %copy.97 = bf16[1,2048,512]{2,0,1:T(2,128)(2,1)} copy(bf16[1,2048,512]{2,1,0:T(8,128)(2,1)S(1)} %bitcast.105) | data formatting | bytes 4194304 | tf_op jit(solution)/shard_map/broadcast_in_dim;reshape | solution.py:109
  279.7 14.0 %reduce.5 = bf16[2048,512]{1,0:T(8,128)(2,1)S(1)} reduce(bf16[2048,1,512]{2,1,0:T(2,128)(2,1)} %bitcast.95, bf16[]{:T(256)} %broadcast.127), dimensions={1}, to_apply=%bitcast.69.reduce_sub_computation | reduce | bytes 4194306
  293.7 2.8 reshape.140
  296.5 7.2 %all-to-all-start.2 = ((bf16[16,2,32768]{2,1,0:T(2,128)(2,1)}), bf16[16,2,32768]{2,1,0:T(2,128)(2,1)S(1)}, u32[]{:S(2)}, u32[]{:S(2)}) async-start(bf16[16,2,32768]{2,1,0:T(2,128)(2,1)} %reshape.140), calls=%async_computation.2 | async-start | bytes 4194304 | tf_op jit(solution)/shard_map/all_to_all | solution.py:109
  303.7 0.3 all-gather.10.cloned.1.call-start
  304.0 0.4 all-gather.10.cloned.1.call-update
  304.4 126.7 %all-gather.10.cloned.1.call-done = bf16[512,2,512]{2,1,0:T(2,128)(2,1)} async-done(((bf16[1,2,512]{2,1,0:T(2,128)(2,1)}), bf16[512,2,512]{2,1,0:T(2,128)(2,1)}) %all-gather.10.cloned.1.call-update) | async-done | bytes 1048592 | tf_op jit(solution)/shard_map/all_gather | solution.py:124
  431.1 1.5 reshape.138
  432.6 2.5 reshape.145
  435.1 2.2 copy.83
  437.4 2.5 reshape.143
  439.9 2.2 copy.81
  442.2 6.8 %reshape.141 = bf16[2048,1,512]{2,1,0:T(2,128)(2,1)} reshape(bf16[16,2,32768]{2,1,0:T(2,128)(2,1)S(1)} %all-to-all-done.2) | data formatting | bytes 4194304
  449.0 4.6 copy_convert_fusion
  453.6 5.5 %copy.88 = f32[1,2048,512]{1,2,0:T(8,128)} copy(f32[1,2048,512]{2,1,0:T(8,128)} %copy_convert_fusion) | data formatting | bytes 8388608 | tf_op jit(solution)/shard_map/convert_element_type | solution.py:113
  459.1 3.1 copy.94
  462.2 1.0 multiply_reduce_fusion
  463.2 1.2 convolution_convert_fusion.1
  (59 shorter events, 1.7 us)
Async XLA Ops:
  6.5 1.4 copy-start
  6.5 127.7 %all-gather.8.cloned.1.call-start = ((), (), s32[]{:S(2)}) async-start(), calls=%async_computation.4 | async-start | bytes 3151872 | tf_op jit(solution)/shard_map/all_gather | solution.py:81
  7.3 174.4 %all-gather.6.cloned.1.call-start = ((), (), s32[]{:S(2)}) async-start(), calls=%async_computation.3 | async-start | bytes 2228224 | tf_op jit(solution)/shard_map/all_gather | solution.py:94
  10.2 143.2 %copy-start.4 = (s32[16]{0:T(128)S(1)}, s32[16]{0:T(128)}, u32[]{:S(2)}) copy-start(s32[16]{0:T(128)} %param.11) | copy-start | bytes 196
  10.2 143.3 %copy-start.3 = (s32[16,24]{1,0:T(8,128)S(1)}, s32[16,24]{1,0:T(8,128)}, u32[]{:S(2)}) copy-start(s32[16,24]{1,0:T(8,128)} %param.10) | copy-start | bytes 4612
  142.2 0.7 copy-start.2
  144.6 12.8 %collective-permute-start = (bf16[128,1024]{1,0:T(8,128)(2,1)S(1)}, bf16[128,1024]{1,0:T(8,128)(2,1)S(1)}, u32[]{:S(2)}, u32[]{:S(2)}) collective-permute-start(bf16[128,1024]{1,0:T(8,128)(2,1)S(1)} %slice.21), channel_id=1, source_target_pairs={{0,16},{16,32},{32,48},{48,64},{64,80},{80,96},{96,112},{112,128},... | collective-permute-start | bytes 786440 | tf_op jit(solution)/shard_map/ppermute | solution.py:17
  147.6 10.6 %collective-permute-start.1 = (bf16[128,1024]{1,0:T(8,128)(2,1)S(1)}, bf16[128,1024]{1,0:T(8,128)(2,1)S(1)}, u32[]{:S(2)}, u32[]{:S(2)}) collective-permute-start(bf16[128,1024]{1,0:T(8,128)(2,1)S(1)} %slice.21), channel_id=1, source_target_pairs={{16,0},{32,16},{48,32},{64,48},{80,64},{96,80},{112,96},{128,112},... | collective-permute-start | bytes 786440 | tf_op jit(solution)/shard_map/ppermute | solution.py:18
  218.2 42.9 %copy-start.1 = (bf16[4,512,512]{2,1,0:T(8,128)(2,1)S(1)}, bf16[4,512,512]{2,1,0:T(8,128)(2,1)}, u32[]{:S(2)}) copy-start(bf16[4,512,512]{2,1,0:T(8,128)(2,1)} %get-tuple-element.51) | copy-start | bytes 6291460
  233.8 20.1 %all-to-all-start.1 = ((bf16[16,2,512]{2,1,0:T(2,128)(2,1)}), bf16[16,2,512]{2,1,0:T(2,128)(2,1)S(1)}, u32[]{:S(2)}, u32[]{:S(2)}) async-start(bf16[16,2,512]{2,1,0:T(2,128)(2,1)} %reshape.144), calls=%async_computation.1 | async-start | bytes 65536 | tf_op jit(solution)/shard_map/all_to_all | solution.py:110
  253.9 42.6 %all-to-all-start = ((bf16[16,2,512]{2,1,0:T(2,128)(2,1)}), bf16[16,2,512]{2,1,0:T(2,128)(2,1)S(1)}, u32[]{:S(2)}, u32[]{:S(2)}) async-start(bf16[16,2,512]{2,1,0:T(2,128)(2,1)} %reshape.142), calls=%async_computation | async-start | bytes 65536 | tf_op jit(solution)/shard_map/all_to_all | solution.py:111
  296.5 145.7 %all-to-all-start.2 = ((bf16[16,2,32768]{2,1,0:T(2,128)(2,1)}), bf16[16,2,32768]{2,1,0:T(2,128)(2,1)S(1)}, u32[]{:S(2)}, u32[]{:S(2)}) async-start(bf16[16,2,32768]{2,1,0:T(2,128)(2,1)} %reshape.140), calls=%async_computation.2 | async-start | bytes 4194304 | tf_op jit(solution)/shard_map/all_to_all | solution.py:109
  303.7 127.5 %all-gather.10.cloned.1.call-start = ((), (), s32[]{:S(2)}) async-start(), calls=%async_computation.5 | async-start | bytes 1050624 | tf_op jit(solution)/shard_map/all_gather | solution.py:124
Sparse Core Ops, SparseCore 0:
  11.5 122.6 all-gather.7
  143.7 37.9 all-gather.5
  308.7 122.4 all-gather.9
where the time goes:
time: 472 us; the launch traced here: 471 us
  waiting for transfers between devices  279 us (59%)
  local copies, waits for them, and re-layouts  80.9 us (17%)
  other arithmetic  51.1 us (11%)
  starting transfers between devices  28.5 us (6%)
  matrix products  17.6 us (4%)
  between operations  13.3 us (3%)
    all_gather x1, waiting for transfers between devices, body(): lax.all_gather(out_weight, ('pb', 'ka'), axis=1, tiled=True)  127 us
    all_gather x1, waiting for transfers between devices, body(): lax.all_gather(qkv_weight, ('pb', 'ka'), axis=0, tiled=True)  124 us
    unnamed x3, other arithmetic  38.5 us
    unnamed x20, local copies, waits for them, and re-layouts  31.1 us
    all_gather x1, waiting for transfers between devices, body(): slab_queries = lax.all_gather(own_queries, 'ka', axis=0, tiled=True)  22.9 us
    another operation x1, local copies, waits for them, and re-layouts, body(): partial_value[None]  18.5 us
  transfers between devices with their start and end apart: 8, of which 5 were waited for; matrix products, arithmetic and copies ran while one was open for 14% of the time, Pallas kernels for 0%

commit v1 on v0

--- a/solution.py
+++ b/solution.py
@@ -91,7 +91,10 @@
     dev_blocks = dev_rows // BLK
     slab_of = (slab_index + jnp.arange(3) - 1) % slab_count
     listed_slot = jnp.arange(neighbours.shape[1])[None, :] < counts[:, None]
-    slab_queries = lax.all_gather(own_queries, "ka", axis=0, tiled=True)
+    nodes = lax.axis_size("ka")
+    all_blocks = tuple((nodes if h == 0 else 1 for h in range(own_queries.ndim)))
+    vec_out = jnp.tile(own_queries, all_blocks)
+    slab_queries = lax.all_to_all(vec_out, "ka", split_axis=0, tiled=True, concat_axis=0)
     near_keys = near[:, :attn_width].reshape(3 * dev_rows, head_count, HD)
     near_values = near[:, attn_width:].reshape(3 * dev_rows, head_count, HD)
     block_ids = (

time: 472 us -> 489 us (1.036)
  waiting for transfers between devices: 279 us -> 289 us
    all_to_all x0 -> x1, waiting for transfers between devices: none -> 32 us  [body(): lax.all_to_all(vec_out, 'ka', split_axis=0, tiled=True, concat_axis=0)]
    all_gather x1 -> x0, waiting for transfers between devices: 22.9 us -> none  [body(): slab_queries = lax.all_gather(own_queries, 'ka', axis=0, tiled=True)]
    unnamed x20 -> x22, local copies, waits for them, and re-layouts: 31.1 us -> 31.1 us
where the time goes in v1:
time: 489 us; the launch traced here: 488 us
  waiting for transfers between devices  289 us (59%)
  local copies, waits for them, and re-layouts  79.3 us (16%)
  other arithmetic  51.1 us (10%)
  starting transfers between devices  32.5 us (7%)
  matrix products  21.8 us (4%)
  between operations  13.6 us (3%)
    all_gather x1, waiting for transfers between devices, body(): lax.all_gather(out_weight, ('pb', 'ka'), axis=1, tiled=True)  127 us
    all_gather x1, waiting for transfers between devices, body(): lax.all_gather(qkv_weight, ('pb', 'ka'), axis=0, tiled=True)  124 us
    unnamed x3, other arithmetic  38.5 us
    all_to_all x1, waiting for transfers between devices, body(): lax.all_to_all(vec_out, 'ka', split_axis=0, tiled=True, concat_axis=0)  32 us
    unnamed x22, local copies, waits for them, and re-layouts  31.1 us
    another operation x1, local copies, waits for them, and re-layouts, body(): partial_value[None]  18.5 us
    dot_general x4, matrix products, attend(): jnp.einsum('hqk,khd->qhd', soft_weights.astype(jnp.bfloat16), near_values...  10.2 us
  transfers between devices with their start and end apart: 8, of which 5 were waited for; matrix products, arithmetic and copies ran while one was open for 14% of the time, Pallas kernels for 0%

profile of v1, /device:TPU:1, one launch (start us, length us, event | category | flops | bytes accessed | tf_op | source)
XLA Modules:
  0.0 487.7 jit_solution(14466848398246503076)
XLA Ops:
  6.5 0.7 all-gather.5.cloned.1.call-update
  7.3 0.7 compare_select_fusion
  7.9 1.6 gather_fusion
  9.5 0.7 compare_and_fusion
  10.2 124.1 %all-gather.5.cloned.1.call-done = bf16[512,2,1536]{2,1,0:T(2,128)(2,1)} async-done(((bf16[1,2,1536]{2,1,0:T(2,128)(2,1)}), bf16[512,2,1536]{2,1,0:T(2,128)(2,1)}) %all-gather.5.cloned.1.call-update) | async-done | bytes 3145744 | tf_op jit(solution)/shard_map/all_gather | solution.py:81
  134.2 6.3 %reshape.144 = bf16[1024,1536]{1,0:T(8,128)(2,1)S(1)} reshape(bf16[512,2,1536]{2,1,0:T(2,128)(2,1)} %all-gather.5.cloned.1.call-done) | data formatting | bytes 6291456
  140.6 1.6 convolution_convert_fusion
  142.2 0.7 copy-done.2
  143.1 1.8 tile.2
  144.8 4.4 all-to-all-start
  149.3 2.8 collective-permute-start
  152.1 5.9 %collective-permute-start.1 = (bf16[128,1024]{1,0:T(8,128)(2,1)S(1)}, bf16[128,1024]{1,0:T(8,128)(2,1)S(1)}, u32[]{:S(2)}, u32[]{:S(2)}) collective-permute-start(bf16[128,1024]{1,0:T(8,128)(2,1)S(1)} %slice.21), channel_id=1, source_target_pairs={{16,0},{32,16},{48,32},{64,48},{80,64},{96,80},{112,96},{128,112},... | collective-permute-start | bytes 786440 | tf_op jit(solution)/shard_map/ppermute | solution.py:18
  158.4 4.0 collective-permute-done
  162.4 0.9 collective-permute-done.1
  163.3 0.8 fusion.26
  164.1 1.2 copy.80
  165.3 0.9 copy.81
  166.2 32.0 %all-to-all-done = bf16[16,128,512]{1,2,0:T(8,128)(2,1)S(1)} async-done(((bf16[16,128,512]{1,2,0:T(8,128)(2,1)}), bf16[16,128,512]{1,2,0:T(8,128)(2,1)S(1)}, u32[]{:S(2)}, u32[]{:S(2)}) %all-to-all-start) | async-done | bytes 2097184 | tf_op jit(solution)/shard_map/all_to_all | solution.py:97
  198.2 2.7 copy.79
  200.9 2.7 reshape_reshape.7
  203.7 1.8 copy.83
  205.5 29.0 %while.14 = (s32[]{:T(128)}, bf16[4,512,512]{2,1,0:T(8,128)(2,1)}, bf16[4,512,8]{1,2,0:T(8,128)(2,1)S(1)}, bf16[4,512,8]{1,2,0:T(8,128)(2,1)S(1)}, pred[4,512,3]...) while((s32[]{:T(128)}, bf16[4,512,512]{2,1,0:T(8,128)(2,1)}, ...), condition=%wide.region_4.5_spmd, body=%wide.region_1.4_spmd.sunk | while | flops 420753408 | bytes 23795300 | solution.py:59
  205.6 2.2 select_reduce_fusion.2
  207.8 1.3 fusion.40
  209.1 2.5 select_convert_fusion.2
  211.9 0.8 constant_dynamic-update-slice_fusion.2
  212.8 2.2 select_reduce_fusion.2
  215.0 1.3 fusion.40
  216.4 2.5 select_convert_fusion.2
  219.1 0.8 constant_dynamic-update-slice_fusion.2
  220.0 2.2 select_reduce_fusion.2
  222.3 1.3 fusion.40
  223.6 2.5 select_convert_fusion.2
  226.4 0.8 constant_dynamic-update-slice_fusion.2
  227.3 2.2 select_reduce_fusion.2
  229.5 1.3 fusion.40
  230.9 2.5 select_convert_fusion.2
  233.6 0.8 constant_dynamic-update-slice_fusion.2
  234.5 0.7 copy.86
  235.2 0.5 broadcast.130
  235.7 12.2 %reduce.6 = bf16[2048,8]{1,0:T(8,128)(2,1)} reduce(bf16[2048,1,8]{2,1,0:T(2,128)(2,1)S(1)} %bitcast.103, bf16[]{:T(256)} %broadcast.130), dimensions={1}, to_apply=%bitcast.59.reduce_sub_computation | reduce | bytes 65538
  247.9 2.2 reshape.151
  250.1 5.0 %all-to-all-start.2 = ((bf16[16,2,512]{2,1,0:T(2,128)(2,1)}), bf16[16,2,512]{2,1,0:T(2,128)(2,1)S(1)}, u32[]{:S(2)}, u32[]{:S(2)}) async-start(bf16[16,2,512]{2,1,0:T(2,128)(2,1)} %reshape.151), calls=%async_computation.2 | async-start | bytes 65536 | tf_op jit(solution)/shard_map/all_to_all | solution.py:113
  255.1 0.7 copy.84
  255.8 12.2 %reduce.7 = bf16[2048,8]{1,0:T(8,128)(2,1)} reduce(bf16[2048,1,8]{2,1,0:T(2,128)(2,1)S(1)} %bitcast.104, bf16[]{:T(256)} %broadcast.130), dimensions={1}, to_apply=%bitcast.57.reduce_sub_computation | reduce | bytes 65538
  268.1 2.2 reshape.149
  270.3 7.2 %all-to-all-start.1 = ((bf16[16,2,512]{2,1,0:T(2,128)(2,1)}), bf16[16,2,512]{2,1,0:T(2,128)(2,1)S(1)}, u32[]{:S(2)}, u32[]{:S(2)}) async-start(bf16[16,2,512]{2,1,0:T(2,128)(2,1)} %reshape.149), calls=%async_computation.1 | async-start | bytes 65536 | tf_op jit(solution)/shard_map/all_to_all | solution.py:114
  277.5 18.5 %copy.99 = bf16[1,2048,512]{2,0,1:T(2,128)(2,1)} copy(bf16[1,2048,512]{2,1,0:T(8,128)(2,1)S(1)} %bitcast.107) | data formatting | bytes 4194304 | tf_op jit(solution)/shard_map/broadcast_in_dim;reshape | solution.py:112
  296.0 14.0 %reduce.5 = bf16[2048,512]{1,0:T(8,128)(2,1)S(1)} reduce(bf16[2048,1,512]{2,1,0:T(2,128)(2,1)} %bitcast.97, bf16[]{:T(256)} %broadcast.130), dimensions={1}, to_apply=%bitcast.71.reduce_sub_computation | reduce | bytes 4194306
  310.0 2.8 reshape.147
  312.8 7.2 %all-to-all-start.3 = ((bf16[16,2,32768]{2,1,0:T(2,128)(2,1)}), bf16[16,2,32768]{2,1,0:T(2,128)(2,1)S(1)}, u32[]{:S(2)}, u32[]{:S(2)}) async-start(bf16[16,2,32768]{2,1,0:T(2,128)(2,1)} %reshape.147), calls=%async_computation.3 | async-start | bytes 4194304 | tf_op jit(solution)/shard_map/all_to_all | solution.py:112
  320.1 0.7 all-gather.7.cloned.1.call-update
  320.8 126.8 %all-gather.7.cloned.1.call-done = bf16[512,2,512]{2,1,0:T(2,128)(2,1)} async-done(((bf16[1,2,512]{2,1,0:T(2,128)(2,1)}), bf16[512,2,512]{2,1,0:T(2,128)(2,1)}) %all-gather.7.cloned.1.call-update) | async-done | bytes 1048592 | tf_op jit(solution)/shard_map/all_gather | solution.py:127
  447.6 1.5 reshape.146
  449.1 2.5 reshape.152
  451.6 2.2 copy.87
  453.9 2.5 reshape.150
  456.4 2.2 copy.85
  458.7 6.8 %reshape.148 = bf16[2048,1,512]{2,1,0:T(2,128)(2,1)} reshape(bf16[16,2,32768]{2,1,0:T(2,128)(2,1)S(1)} %all-to-all-done.3) | data formatting | bytes 4194304
  465.5 4.6 copy_convert_fusion
  470.1 5.5 %copy.92 = f32[1,2048,512]{1,2,0:T(8,128)} copy(f32[1,2048,512]{2,1,0:T(8,128)} %copy_convert_fusion) | data formatting | bytes 8388608 | tf_op jit(solution)/shard_map/convert_element_type | solution.py:116
  475.6 3.1 copy.96
  478.7 1.0 multiply_reduce_fusion
  479.7 1.2 convolution_convert_fusion.1
  (63 shorter events, 2.0 us)
Async XLA Ops:
  6.5 1.4 copy-start
  6.5 127.7 %all-gather.5.cloned.1.call-start = ((), (), s32[]{:S(2)}) async-start(), calls=%async_computation.4 | async-start | bytes 3151872 | tf_op jit(solution)/shard_map/all_gather | solution.py:81
  142.2 0.8 copy-start.2
  142.9 15.0 %copy-start.5 = (s32[16]{0:T(128)S(1)}, s32[16]{0:T(128)}, u32[]{:S(2)}) copy-start(s32[16]{0:T(128)} %param.11) | copy-start | bytes 196
  142.9 15.1 %copy-start.4 = (s32[16,24]{1,0:T(8,128)S(1)}, s32[16,24]{1,0:T(8,128)}, u32[]{:S(2)}) copy-start(s32[16,24]{1,0:T(8,128)} %param.10) | copy-start | bytes 4612
  142.9 6.3 %copy-start.3 = (bf16[128,1536]{1,0:T(8,128)(2,1)S(1)}, bf16[128,1536]{1,0:T(8,128)(2,1)}, u32[]{:S(2)}) copy-start(bf16[128,1536]{1,0:T(8,128)(2,1)} %copy-done.2) | copy-start | bytes 1179652
  144.8 53.4 %all-to-all-start = ((bf16[16,128,512]{1,2,0:T(8,128)(2,1)}), bf16[16,128,512]{1,2,0:T(8,128)(2,1)S(1)}, u32[]{:S(2)}, u32[]{:S(2)}) async-start(bf16[16,128,512]{1,2,0:T(8,128)(2,1)} %tile.2), calls=%async_computation | async-start | bytes 4194304 | tf_op jit(solution)/shard_map/all_to_all | solution.py:97
  149.3 13.1 %collective-permute-start = (bf16[128,1024]{1,0:T(8,128)(2,1)S(1)}, bf16[128,1024]{1,0:T(8,128)(2,1)S(1)}, u32[]{:S(2)}, u32[]{:S(2)}) collective-permute-start(bf16[128,1024]{1,0:T(8,128)(2,1)S(1)} %slice.21), channel_id=1, source_target_pairs={{0,16},{16,32},{32,48},{48,64},{64,80},{80,96},{96,112},{112,128},... | collective-permute-start | bytes 786440 | tf_op jit(solution)/shard_map/ppermute | solution.py:17
  152.1 11.2 %collective-permute-start.1 = (bf16[128,1024]{1,0:T(8,128)(2,1)S(1)}, bf16[128,1024]{1,0:T(8,128)(2,1)S(1)}, u32[]{:S(2)}, u32[]{:S(2)}) collective-permute-start(bf16[128,1024]{1,0:T(8,128)(2,1)S(1)} %slice.21), channel_id=1, source_target_pairs={{16,0},{32,16},{48,32},{64,48},{80,64},{96,80},{112,96},{128,112},... | collective-permute-start | bytes 786440 | tf_op jit(solution)/shard_map/ppermute | solution.py:18
  234.5 43.0 %copy-start.1 = (bf16[4,512,512]{2,1,0:T(8,128)(2,1)S(1)}, bf16[4,512,512]{2,1,0:T(8,128)(2,1)}, u32[]{:S(2)}) copy-start(bf16[4,512,512]{2,1,0:T(8,128)(2,1)} %get-tuple-element.51) | copy-start | bytes 6291460
  250.1 20.1 %all-to-all-start.2 = ((bf16[16,2,512]{2,1,0:T(2,128)(2,1)}), bf16[16,2,512]{2,1,0:T(2,128)(2,1)S(1)}, u32[]{:S(2)}, u32[]{:S(2)}) async-start(bf16[16,2,512]{2,1,0:T(2,128)(2,1)} %reshape.151), calls=%async_computation.2 | async-start | bytes 65536 | tf_op jit(solution)/shard_map/all_to_all | solution.py:113
  270.3 42.6 %all-to-all-start.1 = ((bf16[16,2,512]{2,1,0:T(2,128)(2,1)}), bf16[16,2,512]{2,1,0:T(2,128)(2,1)S(1)}, u32[]{:S(2)}, u32[]{:S(2)}) async-start(bf16[16,2,512]{2,1,0:T(2,128)(2,1)} %reshape.149), calls=%async_computation.1 | async-start | bytes 65536 | tf_op jit(solution)/shard_map/all_to_all | solution.py:114
  312.8 145.8 %all-to-all-start.3 = ((bf16[16,2,32768]{2,1,0:T(2,128)(2,1)}), bf16[16,2,32768]{2,1,0:T(2,128)(2,1)S(1)}, u32[]{:S(2)}, u32[]{:S(2)}) async-start(bf16[16,2,32768]{2,1,0:T(2,128)(2,1)} %reshape.147), calls=%async_computation.3 | async-start | bytes 4194304 | tf_op jit(solution)/shard_map/all_to_all | solution.py:112
  320.1 127.6 %all-gather.7.cloned.1.call-start = ((), (), s32[]{:S(2)}) async-start(), calls=%async_computation.5 | async-start | bytes 1050624 | tf_op jit(solution)/shard_map/all_gather | solution.py:127
Sparse Core Ops, SparseCore 0:
  11.5 122.6 all-gather.4
  325.1 122.5 all-gather.6
